TPU v7x, 32 devices: a whole 2x2x4 slice. The times are simulated.
32 devices in a mesh: rows: 8 (over z, y), grp: 4 (over x, core).
Axes of the slice: x: 2, y: 2, z: 4, core: 2. Of those that a mesh axis runs over, the one named last changes fastest.
Arguments:
- a_vals: bfloat16 [2048, 16384], P(('rows', 'grp')), may hold values from -0.75 to 0.75
- a_cols: int32 [2048, 4], P(('rows', 'grp')), may hold values from 0 to 2047, as said below
- p_vals: bfloat16 [2048, 16384], P(('rows', 'grp')), may hold values from -0.25 to 0.25
- new_rows: int32 [2048], P(('rows', 'grp')), may hold values from 0 to 7, as said below
Outputs:
- a_moved: bfloat16 [2048, 16384], P(('rows', 'grp'))
- coarse: bfloat16 [2048, 768], P(('rows', 'grp'))
Inputs may be any that keep to these rules, and one draw needn't show every extreme that they name: `a_cols`: the first entry of row i is i itself; every entry names a block row whose slab is slab(i) - 1, slab(i) or slab(i) + 1, with any grp index. `new_rows`: the rows of one device go to each rows index either none or exactly 16 at a time, and for each grp index every rows index receives exactly 64 rows.
All inputs are finite; a program needn't handle non-finite values.
Results may differ from a plain program's by a relative error of at most 0.005.
Values may be sent and summed in bfloat16 or wider, within the bound.
No kernel may reach another device: no remote copies, remote signals or barrier semaphores. Data moves between devices by JAX's collectives and lax.ppermute only.
A program may use at most 192 MiB of HBM per device.

v0:
```python
import jax
import jax.numpy as jnp
from jax import lax
from jax.sharding import PartitionSpec as P

B = 64


def extended(block, sides, width):
    for axis, dim in sides:
        count = lax.axis_size(axis)
        forward = [(i, i + 1) for i in range(count - 1)]
        backward = [(target, source) for source, target in forward]
        low = lax.ppermute(
            lax.slice_in_dim(block, block.shape[dim] - width, None, axis=dim), axis, forward
        )
        high = lax.ppermute(lax.slice_in_dim(block, 0, width, axis=dim), axis, backward)
        block = jnp.concatenate([low, block, high], axis=dim)
    return block


def select_rows(picker, source):
    return jnp.dot(picker, source, preferred_element_type=jnp.float32).astype(jnp.bfloat16)


def migrate(a_vals, new_rows):
    row_count, row_width = a_vals.shape
    rows_total = lax.axis_size("rows")
    capacity = max(2, 2 * row_count // rows_total)
    slot_total = rows_total * capacity
    dest_hot = (new_rows[:, None] == jnp.arange(rows_total, dtype=jnp.int32)[None, :]).astype(
        jnp.int32
    )
    ranking = jnp.sum((jnp.cumsum(dest_hot, axis=0) - 1) * dest_hot, axis=1)
    slot_of = new_rows * capacity + ranking
    slot_ids = jnp.arange(slot_total, dtype=jnp.int32)
    sender = (slot_ids[:, None] == slot_of[None, :]).astype(jnp.bfloat16)
    outgoing = select_rows(sender, a_vals)
    filled = jnp.sum(sender, axis=1)
    incoming, flags = (
        lax.all_to_all(
            outgoing.reshape(rows_total, capacity, row_width),
            "rows",
            split_axis=0,
            concat_axis=0,
            tiled=True,
        ),
        lax.all_to_all(
            filled.reshape(rows_total, capacity), "rows", split_axis=0, concat_axis=0, tiled=True
        ),
    )
    flat_flags = flags.reshape(slot_total).astype(jnp.float32)
    position = jnp.cumsum(flat_flags) - 1.0
    flat_rows = incoming.reshape(slot_total, row_width)
    wanted = jnp.arange(row_count, dtype=jnp.float32)
    receiver = ((position[None, :] == wanted[:, None]) & (flat_flags[None, :] > 0.0)).astype(
        jnp.bfloat16
    )
    return select_rows(receiver, flat_rows)


def galerkin(a_vals, a_cols, p_vals):
    row_count, band = a_cols.shape
    slab_width = p_vals.shape[1] // B
    rows_pos = lax.axis_index("rows")
    slab_rows = row_count * lax.axis_size("grp")
    slab_all = lax.all_gather(p_vals, "grp", axis=0, tiled=True)
    padded = extended(slab_all, (("rows", 0),), slab_rows)
    owner_slab = a_cols // slab_rows
    window_slot = owner_slab - rows_pos + 1
    local_row = window_slot * slab_rows + (a_cols - owner_slab * slab_rows)
    gathered = padded[local_row].reshape(row_count, band, B, slab_width)
    blocks = a_vals.reshape(row_count, B, band, B)
    pieces = []
    for offset in range(3):
        kept_mask = (window_slot == offset).astype(jnp.bfloat16)
        masked = blocks * kept_mask[:, None, :, None]
        pieces.append(
            jnp.einsum("jake,jkef->jaf", masked, gathered, preferred_element_type=jnp.float32)
        )
    products = jnp.stack(pieces, axis=2).reshape(row_count * B, 3 * slab_width).astype(jnp.bfloat16)
    own_rows = p_vals.reshape(row_count * B, slab_width)
    partial_sum = lax.dot_general(
        own_rows, products, (((0,), (0,)), ((), ())), preferred_element_type=jnp.float32
    )
    return lax.psum_scatter(partial_sum, "grp", scatter_dimension=0, tiled=True).astype(
        jnp.bfloat16
    )


def local(a_vals, a_cols, p_vals, new_rows):
    coarse = galerkin(a_vals, a_cols, p_vals)
    a_moved = migrate(a_vals, new_rows)
    return (a_moved, coarse)


def solution(mesh):
    in_specs = (
        P(("rows", "grp"), None),
        P(("rows", "grp"), None),
        P(("rows", "grp"), None),
        P(("rows", "grp")),
    )
    out_specs = (P(("rows", "grp"), None), P(("rows", "grp"), None))
    return jax.shard_map(local, mesh=mesh, in_specs=in_specs, out_specs=out_specs, check_vma=False)
```

profile of v0, /device:TPU:0, one launch (start us, length us, event | category | flops | bytes accessed | tf_op | source)
XLA Modules:
  0.0 567.7 jit_solution(2155070878512227861)
XLA Ops:
  7.2 0.7 all-gather.2.cloned.1.call-update
  7.9 62.6 %all-gather.2.cloned.1.call-done = bf16[256,16384]{1,0:T(8,128)(2,1)} async-done(((bf16[64,16384]{1,0:T(8,128)(2,1)}), bf16[256,16384]{1,0:T(8,128)(2,1)}) %all-gather.2.cloned.1.call-update) | async-done | bytes 8388624 | tf_op jit(solution)/shard_map/all_gather | solution.py:67
  70.5 6.6 %collective-permute-start = (bf16[256,16384]{1,0:T(8,128)(2,1)}, bf16[256,16384]{1,0:T(8,128)(2,1)}, u32[]{:S(2)}, u32[]{:S(2)}) collective-permute-start(bf16[256,16384]{1,0:T(8,128)(2,1)} %all-gather.2.cloned.1.call-done), channel_id=1, source_target_pairs={{0,4},{4,8},{8,12},{12,16},{16,20},{20,24},{24,28},{1,5},{5,9},{9,... | collective-permute-start | bytes 25165832 | tf_op jit(solution)/shard_map/ppermute | solution.py:14
  77.1 1.3 collective-permute-start.1
  78.4 0.7 fusion.21
  79.2 0.8 select_reduce_fusion
  80.1 0.7 multiply_add_fusion
  80.8 0.7 all_to_all.12
  81.5 6.7 %all-to-all-start = ((bf16[8,1,16]{2,1,0:T(2,128)(2,1)}), bf16[8,1,16]{2,1,0:T(2,128)(2,1)S(1)}, u32[]{:S(2)}, u32[]{:S(2)}) async-start(bf16[8,1,16]{2,1,0:T(2,128)(2,1)} %all_to_all.12), calls=%async_computation | async-start | bytes 8192 | tf_op jit(solution)/shard_map/all_to_all | solution.py:48
  88.2 0.7 compare_convert_fusion.2
  88.9 0.7 compare_select_fusion
  89.6 4.9 convolution_convert_fusion
  94.7 339.4 %all-to-all-done = bf16[8,1,16]{2,1,0:T(2,128)(2,1)S(1)} async-done(((bf16[8,1,16]{2,1,0:T(2,128)(2,1)}), bf16[8,1,16]{2,1,0:T(2,128)(2,1)S(1)}, u32[]{:S(2)}, u32[]{:S(2)}) %all-to-all-start) | async-done | bytes 288 | tf_op jit(solution)/shard_map/all_to_all | solution.py:48
  434.2 6.6 %all-to-all-start.1 = ((bf16[8,16,16384]{2,1,0:T(8,128)(2,1)}), bf16[8,16,16384]{2,1,0:T(8,128)(2,1)}, u32[]{:S(2)}, u32[]{:S(2)}) async-start(bf16[8,16,16384]{2,1,0:T(8,128)(2,1)} %bitcast.42), calls=%async_computation.1 | async-start | bytes 8388608 | tf_op jit(solution)/shard_map/all_to_all | solution.py:41
  440.9 5.5 reshape.86
  446.4 2.9 reshape.88
  449.6 17.6 %pad_maximum_fusion = bf16[768,16384]{1,0:T(8,128)(2,1)} fusion(bf16[256,16384]{1,0:T(8,128)(2,1)} %collective-permute-done.1, bf16[256,16384]{1,0:T(8,128)(2,1)} %all-gather.2.cloned.1.call-done, bf16[256,16384]{1,0:T(8,128)(2,1)} %collective-permute-done), kind=kLoop, calls=%fused_computation.1 | loop fusion | flops 75497472 | bytes 50331648 | tf_op jit(solution)/shard_map/concatenate | solution.py:18
  467.3 22.2 %gather_fusion = bf16[256,16384]{1,0:T(8,128)(2,1)} fusion(bf16[768,16384]{1,0:T(8,128)(2,1)} %pad_maximum_fusion, s32[1024]{0:T(1024)S(1)} %pad_clamp_fusion), kind=kCustom, calls=%fused_computation | custom fusion | bytes 16778240 | tf_op jit(solution)/shard_map/gather | solution.py:72
  489.4 9.4 %copy.62 = bf16[32,8,64,256]{3,2,1,0:T(8,128)(2,1)} copy(bf16[32,8,64,256]{3,1,2,0:T(8,128)(2,1)} %bitcast.39) | data formatting | bytes 16777216
  498.8 6.7 %fusion.10 = bf16[64,64,1,256]{3,1,0,2:T(8,128)(2,1)S(1)} fusion(bf16[64,4,64,256]{3,2,1,0:T(8,128)(2,1)} %bitcast.43, bf16[64,64,4,64]{3,2,1,0:T(4,128)(2,1)} %reshape.86, bf16[64,4]{1,0:T(8,128)(2,1)S(1)} %copy.51), kind=kOutput, calls=%fused_computation.18 | convolution fusion | flops 538968064 | bytes 12583424 | tf_op jit(solution)/shard_map/jake,jkef->jaf/dot_general | solution.py:79
  505.9 1.2 copy-done.2
  507.0 2.2 fusion.11
  509.3 2.2 fusion.9
  511.5 3.1 pad_maximum_fusion.1
  514.7 12.3 %copy.55 = bf16[64,64,3,256]{3,2,1,0:T(4,128)(2,1)} copy(bf16[64,64,3,256]{3,1,0,2:T(8,128)(2,1)} %pad_maximum_fusion.1) | data formatting | bytes 12582912 | tf_op jit(solution)/shard_map/stack | solution.py:81
  527.0 5.2 copy.63
  532.2 1.8 convolution_bitcast_fusion
  534.0 1.1 copy.60
  535.7 4.2 convolution_convert_fusion.1
  539.9 19.1 %reduce-scatter.4.cloned.1.call-done = f32[64,768]{1,0:T(8,128)} async-done(((f32[256,768]{1,0:T(8,128)}), f32[64,768]{1,0:T(8,128)}) %reduce-scatter.4.cloned.1.call-update) | async-done | bytes 196624
  559.0 1.1 copy.61
  560.1 0.8 copy.56
  (26 shorter events, 1.6 us)
Async XLA Ops:
  7.2 63.4 %all-gather.2.cloned.1.call-start = ((), (), s32[]{:S(2)}) async-start(), calls=%async_computation.3 | async-start | bytes 10485760 | tf_op jit(solution)/shard_map/all_gather | solution.py:67
  70.5 379.1 %collective-permute-start = (bf16[256,16384]{1,0:T(8,128)(2,1)}, bf16[256,16384]{1,0:T(8,128)(2,1)}, u32[]{:S(2)}, u32[]{:S(2)}) collective-permute-start(bf16[256,16384]{1,0:T(8,128)(2,1)} %all-gather.2.cloned.1.call-done), channel_id=1, source_target_pairs={{0,4},{4,8},{8,12},{12,16},{16,20},{20,24},{24,28},{1,5},{5,9},{9,... | collective-permute-start | bytes 25165832 | tf_op jit(solution)/shard_map/ppermute | solution.py:14
  77.1 372.5 %collective-permute-start.1 = (bf16[256,16384]{1,0:T(8,128)(2,1)}, bf16[256,16384]{1,0:T(8,128)(2,1)}, u32[]{:S(2)}, u32[]{:S(2)}) collective-permute-start(bf16[256,16384]{1,0:T(8,128)(2,1)} %all-gather.2.cloned.1.call-done), channel_id=1, source_target_pairs={{4,0},{8,4},{12,8},{16,12},{20,16},{24,20},{28,24},{5,1},{9,5},{13... | collective-permute-start | bytes 25165832 | tf_op jit(solution)/shard_map/ppermute | solution.py:17
  81.5 352.6 %all-to-all-start = ((bf16[8,1,16]{2,1,0:T(2,128)(2,1)}), bf16[8,1,16]{2,1,0:T(2,128)(2,1)S(1)}, u32[]{:S(2)}, u32[]{:S(2)}) async-start(bf16[8,1,16]{2,1,0:T(2,128)(2,1)} %all_to_all.12), calls=%async_computation | async-start | bytes 8192 | tf_op jit(solution)/shard_map/all_to_all | solution.py:48
  434.2 6.7 %copy-start = (bf16[64,16384]{1,0:T(8,128)(2,1)S(1)}, bf16[64,16384]{1,0:T(8,128)(2,1)}, u32[]{:S(2)}) copy-start(bf16[64,16384]{1,0:T(8,128)(2,1)} %param.4) | copy-start | bytes 6291460
  434.2 101.6 %all-to-all-start.1 = ((bf16[8,16,16384]{2,1,0:T(8,128)(2,1)}), bf16[8,16,16384]{2,1,0:T(8,128)(2,1)}, u32[]{:S(2)}, u32[]{:S(2)}) async-start(bf16[8,16,16384]{2,1,0:T(8,128)(2,1)} %bitcast.42), calls=%async_computation.1 | async-start | bytes 8388608 | tf_op jit(solution)/shard_map/all_to_all | solution.py:41
  440.8 118.2 %reduce-scatter.4.cloned.1.call-start = ((), (), s32[]{:S(2)}) async-start(), calls=%async_computation.4 | async-start | bytes 983040
  498.8 7.0 %copy-start.1 = (bf16[32,8,64,256]{3,2,1,0:T(8,128)(2,1)S(1)}, bf16[32,8,64,256]{3,2,1,0:T(8,128)(2,1)}, u32[]{:S(2)}) copy-start(bf16[32,8,64,256]{3,2,1,0:T(8,128)(2,1)} %copy.62) | copy-start | bytes 25165828
  498.8 8.2 %copy-start.2 = (bf16[64,64,4,64]{3,2,1,0:T(4,128)(2,1)S(1)}, bf16[64,64,4,64]{3,2,1,0:T(4,128)(2,1)}, u32[]{:S(2)}) copy-start(bf16[64,64,4,64]{3,2,1,0:T(4,128)(2,1)} %reshape.86) | copy-start | bytes 6291460
Sparse Core Ops, SparseCore 0:
  9.5 60.9 all-gather.1
  535.3 23.6 reduce-scatter.3
where the time goes:
time: 568 us
  waiting for transfers between devices  422 us (74%)
  local copies, waits for them, and re-layouts  63.4 us (11%)
  other arithmetic  24.9 us (4%)
  matrix products  22.1 us (4%)
  starting transfers between devices  21.3 us (4%)
  between operations  14.2 us (2%)
    all_to_all x1, waiting for transfers between devices, migrate(): lax.all_to_all(filled.reshape(rows_total, capacity), 'rows', split_axis=0...  339 us
    all_gather x1, waiting for transfers between devices, galerkin(): slab_all = lax.all_gather(p_vals, 'grp', axis=0, tiled=True)  62.6 us
    gather x1, local copies, waits for them, and re-layouts, galerkin(): gathered = padded[local_row].reshape(row_count, band, B, slab_width)  22.2 us
    unnamed x3, waiting for transfers between devices  19.8 us
    unnamed x11, local copies, waits for them, and re-layouts  19.1 us
    concatenate x1, other arithmetic, extended(): block = jnp.concatenate([low, block, high], axis=dim)  17.6 us
    another operation x1, local copies, waits for them, and re-layouts, galerkin(): jnp.stack(pieces, axis=2).reshape(row_count * B, 3 * slab_width)  12.3 us
  transfers between devices with their start and end apart: 6, of which 3 were waited for; matrix products, arithmetic and copies ran while one was open for 19% of the time, Pallas kernels for 0%

commit v1 on v0

--- a/solution.py
+++ b/solution.py
@@ -4,6 +4,28 @@
 from jax.sharding import PartitionSpec as P
 
 B = 64
+
+
+def in_order(parts, dim):
+    parts = jnp.moveaxis(parts, 0, dim)
+    shape = parts.shape
+    return parts.reshape(*shape[:dim], shape[dim] * shape[dim + 1], *shape[dim + 2 :])
+
+
+def grow_blocks(shard, axis):
+    peers = lax.axis_size(axis)
+    pieces = shard[None]
+    for level in range(peers.bit_length() - 1):
+        stride = 1 << level
+        received = lax.ppermute(pieces, axis, [(i, i ^ stride) for i in range(peers)])
+        both = jnp.stack([pieces, received])
+        upper = lax.axis_index(axis) >> level & 1
+        pieces = jnp.where(upper == 0, both, both[::-1]).reshape(-1, *shard.shape)
+    return pieces
+
+
+def collect(x, axis, dim):
+    return in_order(grow_blocks(x, axis), dim)
 
 
 def extended(block, sides, width):
@@ -64,7 +86,7 @@
     slab_width = p_vals.shape[1] // B
     rows_pos = lax.axis_index("rows")
     slab_rows = row_count * lax.axis_size("grp")
-    slab_all = lax.all_gather(p_vals, "grp", axis=0, tiled=True)
+    slab_all = collect(p_vals, "grp", 0)
     padded = extended(slab_all, (("rows", 0),), slab_rows)
     owner_slab = a_cols // slab_rows
     window_slot = owner_slab - rows_pos + 1

time: 568 us -> 636 us (1.12)
  waiting for transfers between devices: 422 us -> 458 us
  other arithmetic: 24.9 us -> 47.8 us
    ppermute x0 -> x2, waiting for transfers between devices: none -> 95.2 us  [grow_blocks(): lax.ppermute(pieces, axis, [(i, i ^ stride) for i in range(peers)])]
    all_gather x1 -> x0, waiting for transfers between devices: 62.6 us -> none  [galerkin(): slab_all = lax.all_gather(p_vals, 'grp', axis=0, tiled=True)]
    another operation x1 -> x4, other arithmetic: 0.17 us -> 13.9 us  [the longest x3 13.7 us: grow_blocks(): both = jnp.stack([pieces, received])]
    select_n x0 -> x1, other arithmetic: none -> 12.3 us  [grow_blocks(): pieces = jnp.where(upper == 0, both, both[::-1]).reshape(-1, *shard.shape)]
    unnamed x3 -> x2, waiting for transfers between devices: 19.8 us -> 20 us
    unnamed x11 -> x15, local copies, waits for them, and re-layouts: 19.1 us -> 19.1 us
  transfers between devices with their start and end apart: 6 -> 7, of which waited for: 3 -> 4; matrix products, arithmetic and copies ran while one was open for 19% -> 16% of each run, Pallas kernels for 0% -> 0%
where the time goes in v1:
time: 636 us; the launch traced here: 630 us
  waiting for transfers between devices  458 us (72%)
  local copies, waits for them, and re-layouts  63.6 us (10%)
  other arithmetic  47.8 us (8%)
  starting transfers between devices  25.8 us (4%)
  matrix products  20.5 us (3%)
  between operations  14.4 us (2%)
    all_to_all x1, waiting for transfers between devices, migrate(): lax.all_to_all(filled.reshape(rows_total, capacity), 'rows', split_axis=0...  343 us
    ppermute x2, waiting for transfers between devices, grow_blocks(): lax.ppermute(pieces, axis, [(i, i ^ stride) for i in range(peers)])  95.2 us
    gather x1, local copies, waits for them, and re-layouts, galerkin(): gathered = padded[local_row].reshape(row_count, band, B, slab_width)  22.3 us
    unnamed x2, waiting for transfers between devices  20 us
    unnamed x15, local copies, waits for them, and re-layouts  19.1 us
    concatenate x1, other arithmetic, extended(): block = jnp.concatenate([low, block, high], axis=dim)  17.6 us
    another operation x3, other arithmetic, grow_blocks(): both = jnp.stack([pieces, received])  13.7 us
  transfers between devices with their start and end apart: 7, of which 4 were waited for; matrix products, arithmetic and copies ran while one was open for 16% of the time, Pallas kernels for 0%

profile of v1, /device:TPU:0, one launch (start us, length us, event | category | flops | bytes accessed | tf_op | source)
XLA Modules:
  0.0 630.4 jit_solution(4027422215682709605)
XLA Ops:
  7.7 4.0 collective-permute-done
  11.7 2.0 pad_maximum_fusion.3
  13.7 4.3 fusion.10
  18.0 2.8 collective-permute-start.1
  20.8 91.2 %collective-permute-done.1 = bf16[2,64,16384]{2,1,0:T(8,128)(2,1)} collective-permute-done((bf16[2,64,16384]{2,1,0:T(8,128)(2,1)}, bf16[2,64,16384]{2,1,0:T(8,128)(2,1)}, u32[]{:S(2)}, u32[]{:S(2)}) %collective-permute-start.1) | collective-permute-done | bytes 4194336 | tf_op jit(solution)/shard_map/ppermute | solution.py:20
  112.0 7.5 %pad_maximum_fusion.1 = bf16[2,2,64,16384]{3,2,1,0:T(8,128)(2,1)} fusion(bf16[1,2,64,16384]{3,2,1,0:T(8,128)(2,1)} %bitcast.7, bf16[1,2,64,16384]{3,2,1,0:T(8,128)(2,1)} %get-tuple-element.14), kind=kLoop, calls=%fused_computation.5 | loop fusion | flops 4194304 | bytes 16777216 | tf_op jit(solution)/shard_map/stack | solution.py:21
  119.5 12.3 %reverse_select_fusion = bf16[2,2,64,16384]{3,2,1,0:T(8,128)(2,1)} fusion(bf16[2,2,64,16384]{3,2,1,0:T(8,128)(2,1)} %pad_maximum_fusion.1, pred[]{:T(512)S(6)} %eq.67), kind=kLoop, calls=%fused_computation.4 | loop fusion | flops 4194304 | bytes 16777216 | tf_op jit(solution)/shard_map/jit(_where)/select_n | solution.py:23
  131.8 6.9 %collective-permute-start.2 = (bf16[256,16384]{1,0:T(8,128)(2,1)}, bf16[256,16384]{1,0:T(8,128)(2,1)}, u32[]{:S(2)}, u32[]{:S(2)}) collective-permute-start(bf16[256,16384]{1,0:T(8,128)(2,1)} %bitcast.50), channel_id=1, source_target_pairs={{0,4},{4,8},{8,12},{12,16},{16,20},{20,24},{24,28},{1,5},{5,9},{9,... | collective-permute-start | bytes 25165832 | tf_op jit(solution)/shard_map/ppermute | solution.py:36
  138.7 1.3 collective-permute-start.3
  140.4 0.7 all_to_all.12
  141.1 7.0 %all-to-all-start = ((bf16[8,1,16]{2,1,0:T(2,128)(2,1)}), bf16[8,1,16]{2,1,0:T(2,128)(2,1)S(1)}, u32[]{:S(2)}, u32[]{:S(2)}) async-start(bf16[8,1,16]{2,1,0:T(2,128)(2,1)} %all_to_all.12), calls=%async_computation | async-start | bytes 8192 | tf_op jit(solution)/shard_map/all_to_all | solution.py:70
  148.1 3.3 convolution_convert_fusion
  151.6 343.1 %all-to-all-done = bf16[8,1,16]{2,1,0:T(2,128)(2,1)S(1)} async-done(((bf16[8,1,16]{2,1,0:T(2,128)(2,1)}), bf16[8,1,16]{2,1,0:T(2,128)(2,1)S(1)}, u32[]{:S(2)}, u32[]{:S(2)}) %all-to-all-start) | async-done | bytes 288 | tf_op jit(solution)/shard_map/all_to_all | solution.py:70
  494.7 6.7 %all-to-all-start.1 = ((bf16[8,16,16384]{2,1,0:T(8,128)(2,1)}), bf16[8,16,16384]{2,1,0:T(8,128)(2,1)}, u32[]{:S(2)}, u32[]{:S(2)}) async-start(bf16[8,16,16384]{2,1,0:T(8,128)(2,1)} %bitcast.54), calls=%async_computation.1 | async-start | bytes 8388608 | tf_op jit(solution)/shard_map/all_to_all | solution.py:63
  502.0 5.5 reshape.89
  507.5 2.9 reshape.92
  510.7 17.6 %pad_maximum_fusion = bf16[768,16384]{1,0:T(8,128)(2,1)} fusion(bf16[256,16384]{1,0:T(8,128)(2,1)} %collective-permute-done.3, bf16[256,16384]{1,0:T(8,128)(2,1)} %bitcast.52, bf16[256,16384]{1,0:T(8,128)(2,1)} %collective-permute-done.2), kind=kLoop, calls=%fused_computation.1 | loop fusion | flops 75497472 | bytes 50331648 | tf_op jit(solution)/shard_map/concatenate | solution.py:40
  528.4 22.3 %gather_fusion = bf16[256,16384]{1,0:T(8,128)(2,1)} fusion(bf16[768,16384]{1,0:T(8,128)(2,1)} %pad_maximum_fusion, s32[1024]{0:T(1024)S(1)} %pad_clamp_fusion), kind=kCustom, calls=%fused_computation | custom fusion | bytes 16778240 | tf_op jit(solution)/shard_map/gather | solution.py:94
  550.7 9.4 %copy.62 = bf16[32,8,64,256]{3,2,1,0:T(8,128)(2,1)} copy(bf16[32,8,64,256]{3,1,2,0:T(8,128)(2,1)} %bitcast.48) | data formatting | bytes 16777216
  560.1 6.7 %fusion.12 = bf16[64,64,1,256]{3,1,0,2:T(8,128)(2,1)S(1)} fusion(bf16[64,4,64,256]{3,2,1,0:T(8,128)(2,1)} %bitcast.55, bf16[64,64,4,64]{3,2,1,0:T(4,128)(2,1)} %reshape.89, bf16[64,4]{1,0:T(8,128)(2,1)S(1)} %copy.51), kind=kOutput, calls=%fused_computation.24 | convolution fusion | flops 538968064 | bytes 12583424 | tf_op jit(solution)/shard_map/jake,jkef->jaf/dot_general | solution.py:101
  567.1 1.2 copy-done.2
  568.3 2.2 fusion.13
  570.6 2.2 fusion.11
  572.8 3.3 pad_maximum_fusion.2
  576.1 12.3 %copy.55 = bf16[64,64,3,256]{3,2,1,0:T(4,128)(2,1)} copy(bf16[64,64,3,256]{3,1,0,2:T(8,128)(2,1)} %pad_maximum_fusion.2) | data formatting | bytes 12582912 | tf_op jit(solution)/shard_map/stack | solution.py:103
  588.4 5.2 copy.63
  593.7 1.8 convolution_bitcast_fusion
  595.5 1.1 copy.60
  597.2 4.2 convolution_convert_fusion.1
  601.4 20.0 %reduce-scatter.4.cloned.1.call-done = f32[64,768]{1,0:T(8,128)} async-done(((f32[256,768]{1,0:T(8,128)}), f32[64,768]{1,0:T(8,128)}) %reduce-scatter.4.cloned.1.call-update) | async-done | bytes 196624
  621.4 1.1 copy.61
  622.5 0.8 copy.56
  (35 shorter events, 2.9 us)
Async XLA Ops:
  7.2 4.6 collective-permute-start
  18.0 94.0 %collective-permute-start.1 = (bf16[2,64,16384]{2,1,0:T(8,128)(2,1)}, bf16[2,64,16384]{2,1,0:T(8,128)(2,1)}, u32[]{:S(2)}, u32[]{:S(2)}) collective-permute-start(bf16[2,64,16384]{2,1,0:T(8,128)(2,1)} %get-tuple-element.15), channel_id=1, source_target_pairs={{0,2},{1,3},{2,0},{3,1},{4,6},{5,7},{6,4},{7,5},{8,10},{9,11},{10,... | collective-permute-start | bytes 12582920 | tf_op jit(solution)/shard_map/ppermute | solution.py:20
  119.5 20.5 %copy-start.4 = (s32[64]{0:T(128)S(1)}, s32[64]{0:T(128)}, u32[]{:S(2)}) copy-start(s32[64]{0:T(128)} %param.7) | copy-start | bytes 772
  119.5 28.6 %copy-start.3 = (s32[64,4]{0,1:T(4,128)S(1)}, s32[64,4]{0,1:T(4,128)}, u32[]{:S(2)}) copy-start(s32[64,4]{0,1:T(4,128)} %param.5) | copy-start | bytes 3076
  119.5 28.6 %copy-start = (bf16[64,16384]{1,0:T(8,128)(2,1)S(1)}, bf16[64,16384]{1,0:T(8,128)(2,1)}, u32[]{:S(2)}) copy-start(bf16[64,16384]{1,0:T(8,128)(2,1)} %param.4) | copy-start | bytes 6291460
  131.8 378.9 %collective-permute-start.2 = (bf16[256,16384]{1,0:T(8,128)(2,1)}, bf16[256,16384]{1,0:T(8,128)(2,1)}, u32[]{:S(2)}, u32[]{:S(2)}) collective-permute-start(bf16[256,16384]{1,0:T(8,128)(2,1)} %bitcast.50), channel_id=1, source_target_pairs={{0,4},{4,8},{8,12},{12,16},{16,20},{20,24},{24,28},{1,5},{5,9},{9,... | collective-permute-start | bytes 25165832 | tf_op jit(solution)/shard_map/ppermute | solution.py:36
  138.7 372.1 %collective-permute-start.3 = (bf16[256,16384]{1,0:T(8,128)(2,1)}, bf16[256,16384]{1,0:T(8,128)(2,1)}, u32[]{:S(2)}, u32[]{:S(2)}) collective-permute-start(bf16[256,16384]{1,0:T(8,128)(2,1)} %bitcast.51), channel_id=1, source_target_pairs={{4,0},{8,4},{12,8},{16,12},{20,16},{24,20},{28,24},{5,1},{9,5},{13... | collective-permute-start | bytes 25165832 | tf_op jit(solution)/shard_map/ppermute | solution.py:39
  141.1 353.6 %all-to-all-start = ((bf16[8,1,16]{2,1,0:T(2,128)(2,1)}), bf16[8,1,16]{2,1,0:T(2,128)(2,1)S(1)}, u32[]{:S(2)}, u32[]{:S(2)}) async-start(bf16[8,1,16]{2,1,0:T(2,128)(2,1)} %all_to_all.12), calls=%async_computation | async-start | bytes 8192 | tf_op jit(solution)/shard_map/all_to_all | solution.py:70
  494.7 102.5 %all-to-all-start.1 = ((bf16[8,16,16384]{2,1,0:T(8,128)(2,1)}), bf16[8,16,16384]{2,1,0:T(8,128)(2,1)}, u32[]{:S(2)}, u32[]{:S(2)}) async-start(bf16[8,16,16384]{2,1,0:T(8,128)(2,1)} %bitcast.54), calls=%async_computation.1 | async-start | bytes 8388608 | tf_op jit(solution)/shard_map/all_to_all | solution.py:63
  501.5 120.0 %reduce-scatter.4.cloned.1.call-start = ((), (), s32[]{:S(2)}) async-start(), calls=%async_computation.3 | async-start | bytes 983040
  560.1 7.0 %copy-start.1 = (bf16[32,8,64,256]{3,2,1,0:T(8,128)(2,1)S(1)}, bf16[32,8,64,256]{3,2,1,0:T(8,128)(2,1)}, u32[]{:S(2)}) copy-start(bf16[32,8,64,256]{3,2,1,0:T(8,128)(2,1)} %copy.62) | copy-start | bytes 25165828
  560.1 8.2 %copy-start.2 = (bf16[64,64,4,64]{3,2,1,0:T(4,128)(2,1)S(1)}, bf16[64,64,4,64]{3,2,1,0:T(4,128)(2,1)}, u32[]{:S(2)}) copy-start(bf16[64,64,4,64]{3,2,1,0:T(4,128)(2,1)} %reshape.89) | copy-start | bytes 6291460
Sparse Core Ops, SparseCore 0:
  596.8 24.5 reduce-scatter.3
